TPU v7x, 512 devices: a whole 4x4x16 slice. The times are simulated.
512 devices in a mesh: ctx: 64 (over z, x), head: 8 (over y, core).
Axes of the slice: x: 4, y: 4, z: 16, core: 2. Of those that a mesh axis runs over, the one named last changes fastest.
Arguments:
- queries: bfloat16 [16384, 4096], P('ctx', 'head'), may hold values from -4.5 to 4.5
- keys: bfloat16 [16384, 1024], P('ctx', 'head'), may hold values from -4.5 to 4.5
- values: bfloat16 [16384, 1024], P('ctx', 'head'), may hold values from -6 to 6
- out_weight: bfloat16 [4096, 4096], P('head'), may hold values from -0.125 to 0.125
- doc_blocks: int32 [4], replicated, may hold values from 1 to 64, 128 in all
- swap_pairs: int32 [128], replicated, may hold values from 0 to 127, as said below
Outputs:
- mixed: bfloat16 [16384, 4096], P('ctx', 'head')
Inputs may be any that keep to these rules, and one draw needn't show every extreme that they name: swap_pairs[b] is the sequence block held in stored block b (rows b * 128 to b * 128 + 127); the 128 blocks are paired in swaps: swap_pairs[swap_pairs[b]] = b and swap_pairs[b] != b. `doc_blocks`: the lengths sum to 128.
All inputs are finite; a program needn't handle non-finite values.
Results may differ from a plain program's by a relative error of at most 0.018.
Values may be sent and summed in bfloat16 or wider, within the bound.
A program may use at most 64 MiB of HBM per device.

v0:
```python
import jax
import jax.numpy as jnp
from jax import lax
from jax.sharding import PartitionSpec as P

QH = 32
KVH = 8
HD = 128
BLOCK = 128


masked_score = -1e30
step_blocks = 8


def row_lookup(lookup_table, indices):
    matches = indices[:, None] == jnp.arange(lookup_table.shape[0], dtype=jnp.int32)[None, :]
    return jnp.sum(jnp.where(matches, lookup_table[None, :], 0), axis=1)


def doc_tables(doc_blocks, swap_pairs):
    block_count = swap_pairs.shape[0]
    doc_ends = jnp.cumsum(doc_blocks)
    seq_ids = jnp.arange(block_count, dtype=jnp.int32)
    doc_of_seq = jnp.sum((doc_ends[None, :] <= seq_ids[:, None]).astype(jnp.int32), axis=1)
    doc_starts = doc_ends - doc_blocks
    start_of_seq = row_lookup(doc_starts, doc_of_seq)
    return (doc_of_seq, start_of_seq)


def absorb(carry_state, query_heads, key_piece, value_piece, visible, score_scale):
    row_max, denominator, accumulated = carry_state
    scores = (
        jnp.einsum("tkgd,skd->kgts", query_heads, key_piece, preferred_element_type=jnp.float32)
        * score_scale
    )
    scores = jnp.where(visible[None, None], scores, masked_score)
    new_max = jnp.maximum(row_max, jnp.max(scores, axis=-1))
    lifted = jnp.where(visible[None, None], jnp.exp(scores - new_max[..., None]), 0.0)
    shrink = jnp.exp(row_max - new_max)
    weights = lifted.astype(jnp.bfloat16)
    denominator = denominator * shrink + jnp.sum(lifted, axis=-1)
    accumulated = accumulated * shrink[..., None] + jnp.einsum(
        "kgts,skd->kgtd", weights, value_piece, preferred_element_type=jnp.float32
    )
    return (new_max, denominator, accumulated)


def finish(carry_state):
    row_max, denominator, accumulated = carry_state
    return jnp.transpose(accumulated / denominator[..., None], (2, 0, 1, 3)).astype(jnp.bfloat16)


def local(queries, keys, values, out_weight, doc_blocks, swap_pairs):
    block_count = swap_pairs.shape[0]
    tok_rows = queries.shape[0]
    kv_heads = keys.shape[1] // HD
    group_size = QH // KVH
    local_blocks = tok_rows // BLOCK
    score_scale = HD ** (-0.5)
    doc_of_seq, start_of_seq = doc_tables(doc_blocks, swap_pairs)
    first_block = lax.axis_index("ctx") * local_blocks
    query_heads = queries.reshape(tok_rows, kv_heads, group_size, HD)
    row_offsets = jnp.arange(BLOCK, dtype=jnp.int32)
    all_keys, all_values = (
        lax.all_gather(keys, "ctx", axis=0, tiled=True),
        lax.all_gather(values, "ctx", axis=0, tiled=True),
    )
    key_blocks = all_keys.reshape(block_count, BLOCK, kv_heads, HD)
    value_blocks = all_values.reshape(block_count, BLOCK, kv_heads, HD)

    def one_block(local_index):
        storage = first_block + local_index
        seq_block = swap_pairs[storage]
        doc_start = start_of_seq[seq_block]
        block_queries = lax.dynamic_slice_in_dim(query_heads, local_index * BLOCK, BLOCK, 0)
        query_pos = seq_block * BLOCK + row_offsets
        turn_count = (seq_block - doc_start) // step_blocks + 1

        def one_turn(step_index, carry_state):
            wanted = seq_block - step_index * step_blocks - jnp.arange(step_blocks, dtype=jnp.int32)
            usable = wanted >= doc_start
            source = swap_pairs[jnp.maximum(wanted, 0)]
            key_piece = jnp.take(key_blocks, source, axis=0).reshape(
                step_blocks * BLOCK, kv_heads, HD
            )
            value_piece = jnp.take(value_blocks, source, axis=0).reshape(
                step_blocks * BLOCK, kv_heads, HD
            )
            key_pos = (wanted[:, None] * BLOCK + row_offsets[None, :]).reshape(step_blocks * BLOCK)
            key_ok = jnp.repeat(usable, BLOCK)
            visible = key_ok[None, :] & (key_pos[None, :] <= query_pos[:, None])
            return absorb(carry_state, block_queries, key_piece, value_piece, visible, score_scale)

        start_state = (
            jnp.full((kv_heads, group_size, BLOCK), masked_score, jnp.float32),
            jnp.zeros((kv_heads, group_size, BLOCK), jnp.float32),
            jnp.zeros((kv_heads, group_size, BLOCK, HD), jnp.float32),
        )
        return finish(lax.fori_loop(jnp.int32(0), turn_count, one_turn, start_state))

    attended = lax.map(one_block, jnp.arange(local_blocks, dtype=jnp.int32))
    attended = attended.reshape(tok_rows, kv_heads * group_size * HD)
    partial_value = jnp.dot(attended, out_weight, preferred_element_type=jnp.float32)
    return lax.psum_scatter(
        partial_value.astype(jnp.bfloat16), "head", scatter_dimension=1, tiled=True
    )


def solution(mesh):
    in_specs = (P("ctx", "head"), P("ctx", "head"), P("ctx", "head"), P("head", None), P(), P())
    out_specs = P("ctx", "head")
    return jax.shard_map(local, mesh=mesh, in_specs=in_specs, out_specs=out_specs, check_vma=False)
```

profile of v0, /device:TPU:1, one launch (start us, length us, event | category | flops | bytes accessed | tf_op | source)
XLA Modules:
  0.0 525.4 jit_solution(4478240567336196883)
XLA Ops:
  10.8 143.3 %all-gather.3.cloned.1.call-done = bf16[16384,128]{1,0:T(8,128)(2,1)} async-done(((bf16[256,128]{1,0:T(8,128)(2,1)}), bf16[16384,128]{1,0:T(8,128)(2,1)}) %all-gather.3.cloned.1.call-update) | async-done | bytes 4194320 | tf_op jit(solution)/shard_map/all_gather | solution.py:66
  154.1 144.1 %all-gather.5.cloned.1.call-done = bf16[16384,128]{1,0:T(8,128)(2,1)} async-done(((bf16[256,128]{1,0:T(8,128)(2,1)}), bf16[16384,128]{1,0:T(8,128)(2,1)}) %all-gather.5.cloned.1.call-update) | async-done | bytes 4194320 | tf_op jit(solution)/shard_map/all_gather | solution.py:67
  298.2 80.1 %while.43 = (s32[]{:T(128)}, bf16[2,128,1,4,128]{4,3,1,0,2:T(4,128)(2,1)S(1)}, s32[2]{0:T(128)S(1)}, s32[]{:T(128)}, s32[128]{0:T(128)}, /*index=5*/s32[128]{0:T...) while((s32[]{:T(128)}, ...), condition=%wide.region_8.10_spmd.clone.clone, body=%wide.region_3.9_spmd.clone.clone.sunk | while | flops 276042528 | bytes 11595038 | solution.py:102
  306.1 10.6 %while.44 = (s32[]{:T(128)}, f32[1,4,128]{2,1,0:T(4,128)S(1)}, f32[1,4,128]{2,1,0:T(4,128)S(1)}, f32[1,4,128,128]{3,2,1,0:T(8,128)S(1)}, s32[]{:T(128)}, /*index...) while((s32[]{:T(128)}, f32[1,4,128]{2,1,0:T(4,128)S(1)}, ...), condition=%wide.region_7.8_spmd, body=%wide.region_4.7_spmd.sunk | while | flops 275911296 | bytes 10145397 | solution.py:100
  306.7 1.3 gather_fusion
  308.1 2.8 gather_fusion.2
  310.9 2.8 gather_fusion.1
  324.9 53.2 %while.44 = (s32[]{:T(128)}, f32[1,4,128]{2,1,0:T(4,128)S(1)}, f32[1,4,128]{2,1,0:T(4,128)S(1)}, f32[1,4,128,128]{3,2,1,0:T(8,128)S(1)}, s32[]{:T(128)}, /*index...) while((s32[]{:T(128)}, f32[1,4,128]{2,1,0:T(4,128)S(1)}, ...), condition=%wide.region_7.8_spmd, body=%wide.region_4.7_spmd.sunk | while | flops 275911296 | bytes 10145397 | solution.py:100
  325.5 1.3 gather_fusion
  326.8 2.8 gather_fusion.2
  329.6 2.8 gather_fusion.1
  336.2 1.3 gather_fusion
  337.5 2.8 gather_fusion.2
  340.3 2.8 gather_fusion.1
  346.8 1.3 gather_fusion
  348.1 2.8 gather_fusion.2
  350.9 2.8 gather_fusion.1
  357.5 1.3 gather_fusion
  358.8 2.8 gather_fusion.2
  361.6 2.8 gather_fusion.1
  369.4 2.8 gather_fusion.2
  372.2 2.8 gather_fusion.1
  378.4 4.8 convolution_convert_fusion
  383.2 135.6 %reduce-scatter.2.cloned.1.call-done = bf16[256,512]{1,0:T(8,128)(2,1)} async-done(((bf16[256,4096]{1,0:T(8,128)(2,1)}), bf16[256,512]{1,0:T(8,128)(2,1)}) %reduce-scatter.2.cloned.1.call-update) | async-done | bytes 262160 | tf_op jit(solution)/shard_map/reduce_scatter | solution.py:105
  (140 shorter events, 29.7 us)
Async XLA Ops:
  6.5 147.5 %all-gather.3.cloned.1.call-start = ((), (), s32[]{:S(2)}) async-start(), calls=%async_computation.1 | async-start | bytes 4259840 | tf_op jit(solution)/shard_map/all_gather | solution.py:66
  7.3 291.0 %all-gather.5.cloned.1.call-start = ((), (), s32[]{:S(2)}) async-start(), calls=%async_computation.2 | async-start | bytes 4259840 | tf_op jit(solution)/shard_map/all_gather | solution.py:67
  8.0 510.8 %reduce-scatter.2.cloned.1.call-start = ((), (), s32[]{:S(2)}) async-start(), calls=%async_computation.3 | async-start | bytes 2359296 | tf_op jit(solution)/shard_map/reduce_scatter | solution.py:105
Sparse Core Ops, SparseCore 0:
  10.3 143.7 all-gather.2
  157.0 141.1 all-gather.4
  383.3 135.4 reduce-scatter.1
where the time goes:
time: 523 us; the launch traced here: 525 us
  waiting for transfers between devices  424 us (81%)
  local copies, waits for them, and re-layouts  48.4 us (9%)
  loops' own time  14.8 us (3%)
  between operations  13.1 us (3%)
  matrix products  12.4 us (2%)
  other arithmetic  12.1 us (2%)
    all_gather x1, waiting for transfers between devices, local(): lax.all_gather(values, 'ctx', axis=0, tiled=True)  144 us
    all_gather x1, waiting for transfers between devices, local(): lax.all_gather(keys, 'ctx', axis=0, tiled=True)  143 us
    reduce_scatter x1, waiting for transfers between devices, local(): lax.psum_scatter(partial_value.astype(jnp.bfloat16), 'head', scatter_dime...  136 us
    gather x6, local copies, waits for them, and re-layouts, one_turn(): jnp.take(key_blocks, source, axis=0)  16.7 us
    gather x6, local copies, waits for them, and re-layouts, one_turn(): jnp.take(value_blocks, source, axis=0)  16.7 us
  transfers between devices with their start and end apart: 3, of which 3 were waited for; matrix products, arithmetic and copies ran while one was open for 1% of the time, Pallas kernels for 0%

commit v1 on v0

v1 whole, which is shorter than its diff:
```python
import functools

import jax
import jax.numpy as jnp
from jax import lax
from jax.experimental import pallas as pl
from jax.experimental.pallas import tpu as pltpu
from jax.sharding import PartitionSpec as P

HD = 128
BLOCK = 128
NX = 4
NC = 2
SCALE2 = 1.4426950408889634 * HD ** (-0.5)
MASKED = -1e30
MESH = pl.DeviceIdType.MESH
ANY = pl.BlockSpec(memory_space=pl.ANY)
VMEM = pl.BlockSpec(memory_space=pltpu.VMEM)
SMEM = pl.BlockSpec(memory_space=pltpu.SMEM)


def remote(src, dst, send_sem, recv_sem, device):
    return pltpu.make_async_remote_copy(
        src_ref=src,
        dst_ref=dst,
        send_sem=send_sem,
        recv_sem=recv_sem,
        device_id=device,
        device_id_type=MESH,
    )


def greet(devices):
    barrier = pltpu.get_barrier_semaphore()
    for device in devices:
        pl.semaphore_signal(barrier, inc=1, device_id=device, device_id_type=MESH)
    pl.semaphore_wait(barrier, len(devices))


def gather_kernel(nz, q_ref, k_ref, v_ref, q_all, k_all, v_all, vt, ksend, krecv, vsend, vrecv, qsend, qrecv, local_sem):
    ctx = lax.axis_index("ctx")
    head = lax.axis_index("head")
    z, x = ctx // NX, lax.rem(ctx, NX)
    at = lambda zz, xx: (lax.rem(zz + nz, nz) * NX + lax.rem(xx + NX, NX), head)
    up, down = at(z + 1, x), at(z - 1, x)
    right, left = at(z, x + 1), at(z, x - 1)
    vt[...] = v_ref[...].T
    greet([up, down, right, left])
    half = q_ref.shape[0] // 2
    qpart = lambda ref, part: ref.at[pl.ds(part * half, half)]

    def zcopy(array, sends, recvs, own, step, way):
        origin = lax.rem(z - step + nz, nz) if way == 0 else lax.rem(z + step, nz)
        src = own if step == 0 else array.at[origin]
        return remote(
            src, array.at[origin], sends.at[way, step], recvs.at[way, step], up if way == 0 else down
        )

    far = nz // 2
    kc = [[zcopy(k_all, ksend, krecv, k_ref, s, w) for s in range(far if w == 0 else far - 1)] for w in (0, 1)]
    vc = [[zcopy(v_all, vsend, vrecv, vt, s, w) for s in range(far - 1 if w == 0 else far)] for w in (0, 1)]
    for w in (0, 1):
        kc[w][0].start()
    for w in (0, 1):
        vc[w][0].start()

    def qcopy(way, part):
        return remote(
            qpart(q_ref, part), qpart(q_all.at[x], part), qsend.at[way, part], qrecv.at[way, part],
            right if way == 0 else left,
        )

    qc = [[qcopy(0, 0), qcopy(0, 1)], [qcopy(1, 1), qcopy(1, 0)]]
    for i in (0, 1):
        for w in (0, 1):
            qc[w][i].start()
    local = [
        pltpu.make_async_copy(q_ref, q_all.at[x], local_sem.at[0]),
        pltpu.make_async_copy(k_ref, k_all.at[z], local_sem.at[1]),
        pltpu.make_async_copy(vt, v_all.at[z], local_sem.at[2]),
    ]
    for c in local:
        c.start()

    qx = []
    for step in range(far):
        for copies in (kc, vc):
            for w in (0, 1):
                if step < len(copies[w]):
                    copies[w][step].wait_recv()
                    if step + 1 < len(copies[w]):
                        copies[w][step + 1].start()
        if step == 2:
            origins = (lax.rem(x + NX - 1, NX), lax.rem(x + 1, NX))
            for w in (0, 1):
                qc[w][0].wait_recv()
                c = remote(
                    qpart(q_all.at[origins[w]], w), qpart(q_all.at[origins[w]], w),
                    qsend.at[w, 2], qrecv.at[w, 2], right if w == 0 else left,
                )
                c.start()
                qx.append(c)
    for w in (0, 1):
        qc[w][1].wait_recv()
        qx[w].wait_recv()
    for w in (0, 1):
        for c in kc[w] + vc[w] + qc[w] + [qx[w]]:
            c.wait_send()
    for c in local:
        c.wait()


def attend_kernel(nz, swap, docs, q_all, k_all, v_all, o_ref, lse_ref, qt, acc, found):
    ctx = lax.axis_index("ctx")
    z, x = ctx // NX, lax.rem(ctx, NX)
    group = o_ref.shape[1] // HD
    wide = group * BLOCK
    per = q_all.shape[1] // BLOCK
    ndocs = docs.shape[0]
    diff = lax.broadcasted_iota(jnp.int32, (BLOCK, wide), 0) - lax.rem(
        lax.broadcasted_iota(jnp.int32, (BLOCK, wide), 1), BLOCK
    )

    def one_block(qb, _):
        p, t = qb // per, lax.rem(qb, per)
        seq = swap[(z * NX + p) * per + t]
        start = jnp.int32(0)
        end = jnp.int32(0)
        for d in range(ndocs):
            end = end + docs[d]
            start = jnp.where(end <= seq, end, start)

        def look(j, n):
            ks = swap[((j // per) * NX + x) * per + lax.rem(j, per)]
            found[n] = j
            found[64 + n] = (seq - ks) * BLOCK
            return n + ((ks >= start) & (ks <= seq)).astype(jnp.int32)

        count = lax.fori_loop(0, nz * per, look, jnp.int32(0), unroll=4)
        found[count] = jnp.int32(0)
        found[64 + count] = jnp.int32(-(1 << 24))

        rows = pl.ds(pl.multiple_of(t * BLOCK, BLOCK), BLOCK)
        for h in range(group):
            qt[:, h * BLOCK:(h + 1) * BLOCK] = q_all[p, rows, h * HD:(h + 1) * HD].T
        acc[...] = jnp.zeros_like(acc)

        def turn(i, state):
            m, l = state
            scores, vals = [], []
            for e in range(2):
                j = found[2 * i + e]
                limit = found[64 + 2 * i + e]
                piece = pl.ds(pl.multiple_of(lax.rem(j, per) * BLOCK, BLOCK), BLOCK)
                s = jnp.dot(k_all[j // per, piece, :], qt[...], preferred_element_type=jnp.float32)
                scores.append(jnp.where(diff <= limit, s, MASKED))
                vals.append(v_all[j // per, :, piece])
            s = jnp.concatenate(scores, axis=0)
            new = jnp.maximum(m, jnp.max(s, axis=0, keepdims=True))
            shrink = jnp.exp2((m - new) * SCALE2)
            lifted = jnp.exp2((s - new) * SCALE2)
            l = l * shrink + jnp.sum(lifted, axis=0, keepdims=True)
            acc[...] = acc[...] * shrink + jnp.dot(
                jnp.concatenate(vals, axis=1), lifted.astype(jnp.bfloat16), preferred_element_type=jnp.float32
            )
            return new, l

        m, l = lax.fori_loop(
            0, (count + 1) // 2, turn,
            (jnp.full((1, wide), MASKED, jnp.float32), jnp.zeros((1, wide), jnp.float32)),
        )
        some = l > 0.0
        l = jnp.where(some, l, 1.0)
        lse = jnp.where(some, m * SCALE2 + jnp.log2(l), MASKED)
        out = (acc[...] / l).astype(o_ref.dtype)
        for h in range(group):
            o_ref[p, h * HD:(h + 1) * HD, rows] = out[:, h * BLOCK:(h + 1) * BLOCK]
            lse_ref[p, pl.ds(h, 1), rows] = lse[:, h * BLOCK:(h + 1) * BLOCK]
        return 0

    lax.fori_loop(0, NX * per, one_block, 0)


def mix_kernel(
    ny, o_ref, lse_ref, w_ref, out_ref,
    parts, stats, onward, att, given, taken, sums, halves, finals,
    osend, orecv, ssend, srecv, csend, crecv, hsend, hrecv, fsend, frecv,
):
    ctx = lax.axis_index("ctx")
    head = lax.axis_index("head")
    z, x = ctx // NX, lax.rem(ctx, NX)
    y, core = head // NC, lax.rem(head, NC)
    xat = lambda xx: (z * NX + lax.rem(xx + NX, NX), head)
    yat = lambda yy: (ctx, lax.rem(yy + ny, ny) * NC + core)
    right, left, across = xat(x + 1), xat(x - 1), xat(x + 2)
    up, down = yat(y + 1), yat(y - 1)
    twin = (ctx, y * NC + 1 - core)
    greet([right, left, across, up, down, twin])
    xs = [lax.rem(x + 1, NX), lax.rem(x + NX - 1, NX), lax.rem(x + 2, NX)]
    feats, toks = o_ref.shape[1], o_ref.shape[2]
    half = feats // 2
    fpart = lambda ref, part: ref.at[pl.ds(part * half, half)]
    ways = (right, left)

    first = [remote(fpart(o_ref.at[xs[2]], w), onward.at[w], osend.at[2 + w], orecv.at[2 + w], ways[w]) for w in (0, 1)]
    near = [remote(o_ref.at[xs[w]], parts.at[w], osend.at[w], orecv.at[w], ways[w]) for w in (0, 1)]
    small = [
        remote(lse_ref.at[xs[i]], stats.at[i], ssend.at[i], srecv.at[i], (right, left, across)[i]) for i in range(3)
    ]
    for c in small + first + near:
        c.start()
    second = [
        remote(onward.at[w], fpart(parts.at[2], w), osend.at[4 + w], orecv.at[4 + w], ways[w]) for w in (0, 1)
    ]
    for w in (0, 1):
        first[w].wait_recv()
        second[w].start()
    for c in small:
        c.wait_recv()
    own_lse = lse_ref[x]
    lses = [own_lse] + [stats[i] for i in range(3)]
    top = functools.reduce(jnp.maximum, lses)
    shares = [jnp.exp2(v - top) for v in lses]
    total = functools.reduce(jnp.add, shares)
    shares = [v / total for v in shares]
    for c in near:
        c.wait_recv()
    for c in second:
        c.wait_recv()
    for h in range(feats // HD):
        rows = slice(h * HD, (h + 1) * HD)
        mixed = o_ref[x, rows, :].astype(jnp.float32) * shares[0][h:h + 1, :]
        for i in range(3):
            mixed = mixed + parts[i, rows, :].astype(jnp.float32) * shares[1 + i][h:h + 1, :]
        att[:, rows] = mixed.T.astype(jnp.bfloat16)

    cols = out_ref.shape[1]

    def product(yy, cc):
        at = pl.multiple_of((lax.rem(yy + ny, ny) * NC + cc) * cols, cols)
        return jnp.dot(att[...], w_ref[:, pl.ds(at, cols)], preferred_element_type=jnp.float32)

    order = (y + 2, y + 1, y - 1, y)
    twins = []
    for i, yy in enumerate(order):
        given[i] = product(yy, 1 - core).astype(jnp.bfloat16)
        c = remote(given.at[i], taken.at[i], csend.at[i], crecv.at[i], twin)
        c.start()
        twins.append(c)
    tok_half = toks // 2
    tpart = lambda ref, part: ref.at[pl.ds(part * tok_half, tok_half)]
    yways = (up, down)
    hops, lasts = [], []
    for i, yy in enumerate(order):
        mine = product(yy, core)
        twins[i].wait_recv()
        mine = mine + taken[i].astype(jnp.float32)
        if i == 0:
            sums[0] = mine.astype(jnp.bfloat16)
            for w in (0, 1):
                c = remote(tpart(sums.at[0], w), halves.at[w], hsend.at[w], hrecv.at[w], yways[w])
                c.start()
                hops.append(c)
        elif i < 3:
            w = i - 1
            hops[w].wait_recv()
            if w == 0:
                sums[i, :tok_half] = (mine[:tok_half] + halves[w].astype(jnp.float32)).astype(jnp.bfloat16)
                sums[i, tok_half:] = mine[tok_half:].astype(jnp.bfloat16)
            else:
                sums[i, :tok_half] = mine[:tok_half].astype(jnp.bfloat16)
                sums[i, tok_half:] = (mine[tok_half:] + halves[w].astype(jnp.float32)).astype(jnp.bfloat16)
            c = remote(sums.at[i], finals.at[w], fsend.at[w], frecv.at[w], yways[w])
            c.start()
            lasts.append(c)
        else:
            for c in lasts:
                c.wait_recv()
            out_ref[...] = (mine + finals[0].astype(jnp.float32) + finals[1].astype(jnp.float32)).astype(out_ref.dtype)
    for c in small + first + near + second + twins + hops + lasts:
        c.wait_send()


def local(queries, keys, values, out_weight, doc_blocks, swap_pairs, nz, ny):
    toks, feats = queries.shape
    dma = pltpu.SemaphoreType.DMA
    bf = jnp.bfloat16
    far = nz // 2
    q_all, k_all, v_all = pl.pallas_call(
        functools.partial(gather_kernel, nz),
        out_shape=(
            jax.ShapeDtypeStruct((NX, toks, feats), bf),
            jax.ShapeDtypeStruct((nz, toks, HD), bf),
            jax.ShapeDtypeStruct((nz, HD, toks), bf),
        ),
        in_specs=[ANY, ANY, VMEM],
        out_specs=(ANY, ANY, ANY),
        scratch_shapes=[
            pltpu.VMEM((HD, toks), bf),
            dma((2, far)), dma((2, far)), dma((2, far)), dma((2, far)),
            dma((2, 3)), dma((2, 3)), dma((3,)),
        ],
        compiler_params=pltpu.CompilerParams(collective_id=0, has_side_effects=True),
        name="gather",
    )(queries, keys, values)

    partial, lse = pl.pallas_call(
        functools.partial(attend_kernel, nz),
        out_shape=(
            jax.ShapeDtypeStruct((NX, feats, toks), bf),
            jax.ShapeDtypeStruct((NX, 8, toks), jnp.float32),
        ),
        in_specs=[SMEM, SMEM, VMEM, VMEM, VMEM],
        out_specs=(VMEM, VMEM),
        scratch_shapes=[
            pltpu.VMEM((HD, feats), bf),
            pltpu.VMEM((HD, feats), jnp.float32),
            pltpu.SMEM((128,), jnp.int32),
        ],
        compiler_params=pltpu.CompilerParams(vmem_limit_bytes=40 << 20),
        name="attend",
    )(swap_pairs, doc_blocks, q_all, k_all, v_all)

    cols = out_weight.shape[1] // (ny * NC)
    return pl.pallas_call(
        functools.partial(mix_kernel, ny),
        out_shape=jax.ShapeDtypeStruct((toks, cols), bf),
        in_specs=[VMEM, VMEM, VMEM],
        out_specs=VMEM,
        scratch_shapes=[
            pltpu.VMEM((3, feats, toks), bf),
            pltpu.VMEM((3, 8, toks), jnp.float32),
            pltpu.VMEM((2, feats // 2, toks), bf),
            pltpu.VMEM((toks, feats), bf),
            pltpu.VMEM((4, toks, cols), bf),
            pltpu.VMEM((4, toks, cols), bf),
            pltpu.VMEM((3, toks, cols), bf),
            pltpu.VMEM((2, toks // 2, cols), bf),
            pltpu.VMEM((2, toks, cols), bf),
            dma((6,)), dma((6,)), dma((3,)), dma((3,)), dma((4,)), dma((4,)),
            dma((2,)), dma((2,)), dma((2,)), dma((2,)),
        ],
        compiler_params=pltpu.CompilerParams(
            collective_id=1, has_side_effects=True, vmem_limit_bytes=48 << 20
        ),
        name="mix",
    )(partial, lse, out_weight)


def solution(mesh):
    nz = mesh.shape["ctx"] // NX
    ny = mesh.shape["head"] // NC
    in_specs = (P("ctx", "head"), P("ctx", "head"), P("ctx", "head"), P("head", None), P(), P())
    return jax.shard_map(
        functools.partial(local, nz=nz, ny=ny),
        mesh=mesh, in_specs=in_specs, out_specs=P("ctx", "head"), check_vma=False,
    )
```

time: 523 us -> 108 us (0.21)
  the two profiles are of different devices: /device:TPU:1 before, /device:TPU:96 now
where the time goes in v1:
time: 108 us
  Pallas kernels  99.9 us (92%)
  local copies, waits for them, and re-layouts  7.86 us (7%)
    pallas_call x1, Pallas kernels, local(): pl.pallas_call(functools.partial(gather_kernel, nz), out_shape=(jax.Shape...  44.3 us
    pallas_call x1, Pallas kernels, local(): pl.pallas_call(functools.partial(mix_kernel, ny), out_shape=jax.ShapeDtyp...  36.6 us
    pallas_call x1, Pallas kernels, local(): pl.pallas_call(functools.partial(attend_kernel, nz), out_shape=(jax.Shape...  19 us
    unnamed x13, local copies, waits for them, and re-layouts  7.86 us

profile of v1, /device:TPU:96, one launch (start us, length us, event | category | flops | bytes accessed | tf_op | source)
XLA Modules:
  0.0 107.8 jit_solution(18189678115328277886)
XLA Ops:
  0.0 44.3 %gather.1 = (bf16[4,256,512]{2,1,0:T(8,128)(2,1)}, bf16[16,256,128]{2,1,0:T(8,128)(2,1)}, bf16[16,128,256]{2,1,0:T(8,128)(2,1)}) custom-call(bf16[256,512]{1,0:T(8,128)(2,1)} %q_ref.1, bf16[256,128]{1,0:T(8,128)(2,1)} %k_ref.1, bf16[256,128]{1,0:T(8,128)(2,1)} %v_ref.1), custom_call_target="tpu_custom_call" | custom-call | tf_op jit(solution)/shard_map/gather/pallas_call | solution.py:289
  44.3 0.0 copy-start.1
  44.3 1.2 %copy-done.1 = bf16[4,256,512]{2,1,0:T(8,128)(2,1)S(1)} copy-done((bf16[4,256,512]{2,1,0:T(8,128)(2,1)S(1)}, bf16[4,256,512]{2,1,0:T(8,128)(2,1)}, u32[]{:S(2)}) %copy-start.1) | copy-done | bytes 1048600
  45.5 0.0 copy-start.2
  45.5 1.2 %copy-done.2 = bf16[16,256,128]{2,1,0:T(8,128)(2,1)S(1)} copy-done((bf16[16,256,128]{2,1,0:T(8,128)(2,1)S(1)}, bf16[16,256,128]{2,1,0:T(8,128)(2,1)}, u32[]{:S(2)}) %copy-start.2) | copy-done | bytes 1048600
  46.8 0.0 copy-start.3
  46.8 1.2 %copy-done.3 = bf16[16,128,256]{2,1,0:T(8,128)(2,1)S(1)} copy-done((bf16[16,128,256]{2,1,0:T(8,128)(2,1)S(1)}, bf16[16,128,256]{2,1,0:T(8,128)(2,1)}, u32[]{:S(2)}) %copy-start.3) | copy-done | bytes 1048600
  48.0 0.0 copy-start.4
  48.0 0.7 copy-done.4
  48.7 0.0 copy-start.5
  48.7 0.7 copy-done.5
  49.3 19.0 %attend.1 = (bf16[4,512,256]{2,1,0:T(8,128)(2,1)S(1)}, f32[4,8,256]{2,1,0:T(8,128)S(1)}) custom-call(s32[128]{0:T(128)S(1)} %copy-done.4, s32[4]{0:T(128)S(1)} %copy-done.5, bf16[4,256,512]{2,1,0:T(8,128)(2,1)S(1)} %copy-done.1, bf16[16,256,128]{2,1,0:T(8,128)(2,1)S(1)} %copy-done.2, bf16[16,128,256]{2,1,0:T(8,128)(2,1)S(1)} %copy-done.3), custom_call_target="tpu_custom_call" | custom-call | tf_op jit(solution)/shard_map/attend/pallas_call | solution.py:307
  68.3 0.0 copy-start
  68.3 2.2 %copy-done = bf16[512,4096]{1,0:T(8,128)(2,1)S(1)} copy-done((bf16[512,4096]{1,0:T(8,128)(2,1)S(1)}, bf16[512,4096]{1,0:T(8,128)(2,1)}, u32[]{:S(2)}) %copy-start) | copy-done | bytes 4194328
  70.5 36.6 %mix.1 = bf16[256,512]{1,0:T(8,128)(2,1)S(1)} custom-call(bf16[4,512,256]{2,1,0:T(8,128)(2,1)S(1)} %get-tuple-element.13.o_ref, f32[4,8,256]{2,1,0:T(8,128)S(1)} %get-tuple-element.14.lse_ref, bf16[512,4096]{1,0:T(8,128)(2,1)S(1)} %copy-done), custom_call_target="tpu_custom_call" | custom-call | tf_op jit(solution)/shard_map/mix/pallas_call | solution.py:325
  107.1 0.7 copy.8
Async XLA Ops:
  44.3 1.2 %copy-start.1 = (bf16[4,256,512]{2,1,0:T(8,128)(2,1)S(1)}, bf16[4,256,512]{2,1,0:T(8,128)(2,1)}, u32[]{:S(2)}) copy-start(bf16[4,256,512]{2,1,0:T(8,128)(2,1)} %get-tuple-element.10.q_all) | copy-start | bytes 3145732
  45.5 1.2 %copy-start.2 = (bf16[16,256,128]{2,1,0:T(8,128)(2,1)S(1)}, bf16[16,256,128]{2,1,0:T(8,128)(2,1)}, u32[]{:S(2)}) copy-start(bf16[16,256,128]{2,1,0:T(8,128)(2,1)} %get-tuple-element.11.k_all) | copy-start | bytes 3145732
  46.8 1.2 %copy-start.3 = (bf16[16,128,256]{2,1,0:T(8,128)(2,1)S(1)}, bf16[16,128,256]{2,1,0:T(8,128)(2,1)}, u32[]{:S(2)}) copy-start(bf16[16,128,256]{2,1,0:T(8,128)(2,1)} %get-tuple-element.12.v_all) | copy-start | bytes 3145732
  48.0 0.7 copy-start.4
  48.7 0.7 copy-start.5
  68.3 2.2 %copy-start = (bf16[512,4096]{1,0:T(8,128)(2,1)S(1)}, bf16[512,4096]{1,0:T(8,128)(2,1)}, u32[]{:S(2)}) copy-start(bf16[512,4096]{1,0:T(8,128)(2,1)} %w_ref.1) | copy-start | bytes 12582916

commit v2 on v0

v2 whole, which is shorter than its diff:
```python
import functools

import jax
import jax.numpy as jnp
from jax import lax
from jax.experimental import pallas as pl
from jax.experimental.pallas import tpu as pltpu
from jax.sharding import PartitionSpec as P

HD = 128
BLOCK = 128
NX = 4
NC = 2
PER = 2
ONES = 16
SCALE2 = 1.4426950408889634 * HD ** (-0.5)
MASKED = -1e30
MESH = pl.DeviceIdType.MESH
ANY = pl.BlockSpec(memory_space=pl.ANY)
VMEM = pl.BlockSpec(memory_space=pltpu.VMEM)
SMEM = pl.BlockSpec(memory_space=pltpu.SMEM)


def layer_kernel(
    nz, ny,
    swap, docs, q_ref, k_ref, v_ref, w_ref, out_ref,
    q_in, v_in, w_all, k_all, v_all, qt, acc, tops,
    o_give, o_take, s_give, s_take, att, given, taken, sums, finals,
    lsem, zsend, zrecv, vsend, vrecv, ksend, krecv, qsend, qrecv,
    osend, orecv, ssend, srecv, csend, crecv, ysend, yrecv,
):
    ctx = lax.axis_index("ctx")
    head = lax.axis_index("head")
    z, x = ctx // NX, lax.rem(ctx, NX)
    y, core = head // NC, lax.rem(head, NC)
    xk = NX - 1 - x
    xq = x + 1 - 2 * lax.rem(x, 2)
    zat = lambda zz: lax.rem(zz + nz, nz)
    yat = lambda yy: lax.rem(yy + ny, ny)
    up = (zat(z + 1) * NX + x, head)
    down = (zat(z - 1) * NX + x, head)
    key_mate = (z * NX + xk, head)
    query_mate = (z * NX + xq, head)
    twin = (ctx, y * NC + 1 - core)
    ydev = lambda yy: (ctx, yat(yy) * NC + core)
    hops = (2, 1, 3)
    far = nz // 2
    group = qt.shape[2] // BLOCK
    cols = out_ref.shape[1]

    def remote(src, dst, send_sem, recv_sem, device):
        return pltpu.make_async_remote_copy(
            src_ref=src, dst_ref=dst, send_sem=send_sem, recv_sem=recv_sem, device_id=device, device_id_type=MESH
        )

    barrier = pltpu.get_barrier_semaphore()
    friends = [up, down, key_mate, query_mate, twin] + [ydev(y + d) for d in hops]
    for device in friends:
        pl.semaphore_signal(barrier, inc=1, device_id=device, device_id_type=MESH)

    loads = [
        pltpu.make_async_copy(v_ref, v_in, lsem.at[0]),
        pltpu.make_async_copy(q_ref, q_in, lsem.at[1]),
        pltpu.make_async_copy(k_ref, k_all.at[z, 0], lsem.at[2]),
        pltpu.make_async_copy(w_ref, w_all, lsem.at[3]),
    ]
    for c in loads:
        c.start()
    loads[0].wait()
    v_all[z, 0] = v_in[...].T
    loads[1].wait()
    for t in range(PER):
        for h in range(group):
            qt[t, :, h * BLOCK:(h + 1) * BLOCK] = q_in[t * BLOCK:(t + 1) * BLOCK, h * HD:(h + 1) * HD].T
    loads[2].wait()
    pl.semaphore_wait(barrier, len(friends))

    def zcopy(stream, way, step):
        origin = zat(z - step) if way == 0 else zat(z + step)
        ref = v_all.at[origin, 0] if stream == 0 else k_all.at[origin, stream - 1]
        return remote(ref, ref, zsend.at[stream, way, step], zrecv.at[stream, way, step], up if way == 0 else down)

    def vcopy(slot, origin):
        return remote(v_all.at[origin, 0], v_all.at[origin, 1], vsend.at[slot], vrecv.at[slot], key_mate)

    kmate = remote(k_all.at[z, 0], k_all.at[z, 1], ksend, krecv, key_mate)
    qmate = [remote(qt.at[t], qt.at[PER + t], qsend.at[t], qrecv.at[t], query_mate) for t in range(PER)]
    vown = vcopy(2 * far, z)
    kmate.start()
    for stream in (0, 1):
        for way in (0, 1):
            zcopy(stream, way, 0).start()
    for c in qmate:
        c.start()
    vown.start()

    seqs, starts = [], []
    for j in range(2 * PER):
        seq = swap[(z * NX + (x if j < PER else xq)) * PER + j % PER]
        start = jnp.int32(0)
        end = jnp.int32(0)
        for d in range(docs.shape[0]):
            end = end + docs[d]
            start = jnp.where(end <= seq, end, start)
        seqs.append(seq)
        starts.append(start)

    acc[...] = jnp.zeros_like(acc)
    tops[...] = jnp.full_like(tops, MASKED)
    wide = group * BLOCK
    causal = lax.broadcasted_iota(jnp.int32, (BLOCK, wide), 0) <= lax.rem(
        lax.broadcasted_iota(jnp.int32, (BLOCK, wide), 1), BLOCK
    )

    def absorb(j, chunks, diagonal=False):
        rows, offsets = [], []
        old = tops[j]
        new = old
        for origin, column in chunks:
            s = jnp.dot(k_all[origin, column], qt[j], preferred_element_type=jnp.float32)
            for b in range(PER):
                ks = swap[(origin * NX + (x if column == 0 else xk)) * PER + b]
                seen = (ks >= starts[j]) & (ks <= seqs[j])
                offset = jnp.where(seen, 0.0, MASKED).astype(jnp.float32)
                part = s[b * BLOCK:(b + 1) * BLOCK]
                if diagonal and b == j:
                    part = jnp.where(causal, part, MASKED)
                new = jnp.maximum(new, jnp.max(part, axis=0, keepdims=True) + offset)
                rows.append(part)
                offsets.append(offset)
        level = new * SCALE2
        weights = [
            jnp.exp2(part * SCALE2 - (level - offset)).astype(jnp.bfloat16) for part, offset in zip(rows, offsets)
        ]
        vals = jnp.concatenate([v_all[origin, column] for origin, column in chunks], axis=1)
        vals = jnp.concatenate([vals, jnp.ones((ONES, vals.shape[1]), jnp.bfloat16)], axis=0)
        product = jnp.dot(vals, jnp.concatenate(weights, axis=0), preferred_element_type=jnp.float32)
        acc[j] = acc[j] * jnp.exp2((old - new) * SCALE2) + product
        tops[j] = new

    def row(s, ways=(0, 1)):
        return [(zat(z - 1 - s) if w == 0 else zat(z + 1 + s), c) for w in ways for c in (0, 1)]

    def arrive(s, ways, onward):
        for stream in (0, 1, 2):
            for w in ways:
                zcopy(stream, w, s).wait_recv()
                if w in onward:
                    zcopy(stream, w, s + 1).start()
                if stream == 0:
                    vcopy(w * far + s, zat(z - 1 - s) if w == 0 else zat(z + 1 + s)).start()

    def mate_values(s, ways=(0, 1)):
        for w in ways:
            vcopy(w * far + s, z).wait_recv()

    own, other = range(PER), range(PER, 2 * PER)
    for j in own:
        absorb(j, [(z, 0)], diagonal=True)
    kmate.wait_recv()
    for w in (0, 1):
        zcopy(2, w, 0).start()
    arrive(0, (0, 1), (0, 1))
    vown.wait_recv()
    for j in own:
        absorb(j, [(z, 1)])
    arrive(1, (0, 1), (0, 1))
    mate_values(0)
    for j in own:
        absorb(j, row(0))
    for c in qmate:
        c.wait_recv()
    for j in other:
        absorb(j, [(z, 0), (z, 1)] + row(0))

    def step(s, _):
        arrive(s, (0, 1), (0, 1))
        mate_values(s - 1)
        for j in range(2 * PER):
            absorb(j, row(s - 1))
        return 0

    lax.fori_loop(2, far - 2, step, 0)
    arrive(far - 2, (0, 1), (0,))
    mate_values(far - 3)
    for j in range(2 * PER):
        absorb(j, row(far - 3))
    arrive(far - 1, (0,), ())
    mate_values(far - 2)
    for j in range(2 * PER):
        absorb(j, row(far - 2))
    mate_values(far - 1, (0,))

    ocopy = [remote(o_give.at[t], o_take.at[t], osend.at[t], orecv.at[t], query_mate) for t in range(PER)]
    scopy = [remote(s_give.at[t], s_take.at[t], ssend.at[t], srecv.at[t], query_mate) for t in range(PER)]
    for t in range(PER):
        j = PER + t
        absorb(j, row(far - 1, (0,)))
        total = acc[j, HD:HD + 1, :]
        some = total > 0.0
        total = jnp.where(some, total, 1.0)
        s_give[t] = jnp.where(some, tops[j] * SCALE2 + jnp.log2(total), MASKED)
        o_give[t] = (acc[j, :HD, :] / total).astype(jnp.bfloat16)
        scopy[t].start()
        ocopy[t].start()
    for j in own:
        absorb(j, row(far - 1, (0,)))

    def product(t, yy, cc):
        at = pl.multiple_of((yat(yy) * NC + cc) * cols, cols)
        return jnp.dot(
            att[t * BLOCK:(t + 1) * BLOCK, :], w_all[:, pl.ds(at, cols)], preferred_element_type=jnp.float32
        )

    order = hops + (0,)
    ccopy = [
        [remote(given.at[t, i], taken.at[t, i], csend.at[t, i], crecv.at[t, i], twin) for i in range(ny)]
        for t in range(PER)
    ]
    ycopy = [
        [
            remote(sums.at[t, i], finals.at[t, i], ysend.at[t, i], yrecv.at[t, i], ydev(y + d))
            for i, d in enumerate(hops)
        ]
        for t in range(PER)
    ]
    loads[3].wait()
    kept = []
    for t in range(PER):
        level = tops[t] * SCALE2
        total = acc[t, HD:HD + 1, :]
        scopy[t].wait_recv()
        ocopy[t].wait_recv()
        theirs = s_take[t]
        top = jnp.maximum(level + jnp.log2(total), theirs)
        mine = jnp.exp2(level - top)
        part = jnp.exp2(theirs - top)
        whole = mine * total + part
        mine, part = mine / whole, part / whole
        mixed = acc[t, :HD, :] * mine + o_take[t].astype(jnp.float32) * part
        for h in range(group):
            att[t * BLOCK:(t + 1) * BLOCK, h * HD:(h + 1) * HD] = (
                mixed[:, h * BLOCK:(h + 1) * BLOCK].T.astype(jnp.bfloat16)
            )
        for i, d in enumerate(order):
            given[t, i] = product(t, y + d, 1 - core).astype(jnp.bfloat16)
            ccopy[t][i].start()
        for i, d in enumerate(order):
            total = product(t, y + d, core)
            ccopy[t][i].wait_recv()
            total = total + taken[t, i].astype(jnp.float32)
            if d:
                sums[t, i] = total.astype(jnp.bfloat16)
                ycopy[t][i].start()
            else:
                kept.append(total)
    for t in range(PER):
        total = kept[t]
        for i in range(len(hops)):
            ycopy[t][i].wait_recv()
            total = total + finals[t, i].astype(jnp.float32)
        out_ref[t * BLOCK:(t + 1) * BLOCK, :] = total.astype(out_ref.dtype)

    kmate.wait_send()
    vown.wait_send()
    for c in qmate + ocopy + scopy + ccopy[0] + ccopy[1] + ycopy[0] + ycopy[1]:
        c.wait_send()

    def left(s, _):
        for stream in (0, 1, 2):
            for w in (0, 1):
                zcopy(stream, w, s).wait_send()
        for w in (0, 1):
            vcopy(w * far + s, z).wait_send()
        return 0

    lax.fori_loop(0, far - 1, left, 0)
    for stream in (0, 1, 2):
        zcopy(stream, 0, far - 1).wait_send()
    vcopy(far - 1, z).wait_send()


def local(queries, keys, values, out_weight, doc_blocks, swap_pairs, nz, ny):
    toks, feats = queries.shape
    dma = pltpu.SemaphoreType.DMA
    bf = jnp.bfloat16
    f32 = jnp.float32
    far = nz // 2
    cols = out_weight.shape[1] // (ny * NC)
    return pl.pallas_call(
        functools.partial(layer_kernel, nz, ny),
        out_shape=jax.ShapeDtypeStruct((toks, cols), bf),
        in_specs=[SMEM, SMEM, ANY, ANY, ANY, ANY],
        out_specs=VMEM,
        scratch_shapes=[
            pltpu.VMEM((toks, feats), bf),
            pltpu.VMEM((toks, HD), bf),
            pltpu.VMEM(out_weight.shape, bf),
            pltpu.VMEM((nz, 2, toks, HD), bf),
            pltpu.VMEM((nz, 2, HD, toks), bf),
            pltpu.VMEM((2 * PER, HD, feats), bf),
            pltpu.VMEM((2 * PER, HD + ONES, feats), f32),
            pltpu.VMEM((2 * PER, 1, feats), f32),
            pltpu.VMEM((PER, HD, feats), bf),
            pltpu.VMEM((PER, HD, feats), bf),
            pltpu.VMEM((PER, 1, feats), f32),
            pltpu.VMEM((PER, 1, feats), f32),
            pltpu.VMEM((toks, feats), bf),
            pltpu.VMEM((PER, ny, BLOCK, cols), bf),
            pltpu.VMEM((PER, ny, BLOCK, cols), bf),
            pltpu.VMEM((PER, ny - 1, BLOCK, cols), bf),
            pltpu.VMEM((PER, ny - 1, BLOCK, cols), bf),
            dma((4,)), dma((3, 2, far)), dma((3, 2, far)), dma((2 * far + 1,)), dma((2 * far + 1,)),
            dma, dma, dma((PER,)), dma((PER,)),
            dma((PER,)), dma((PER,)), dma((PER,)), dma((PER,)),
            dma((PER, ny)), dma((PER, ny)), dma((PER, ny - 1)), dma((PER, ny - 1)),
        ],
        compiler_params=pltpu.CompilerParams(
            collective_id=0, has_side_effects=True, vmem_limit_bytes=56 << 20
        ),
        name="layer",
    )(swap_pairs, doc_blocks, queries, keys, values, out_weight)


def solution(mesh):
    nz = mesh.shape["ctx"] // NX
    ny = mesh.shape["head"] // NC
    in_specs = (P("ctx", "head"), P("ctx", "head"), P("ctx", "head"), P("head", None), P(), P())
    return jax.shard_map(
        functools.partial(local, nz=nz, ny=ny),
        mesh=mesh, in_specs=in_specs, out_specs=P("ctx", "head"), check_vma=False,
    )
```

time: 523 us -> 84.7 us (0.16)
  waiting for transfers between devices: 424 us -> 0 us
  Pallas kernels: 0 us -> 82.9 us
  local copies, waits for them, and re-layouts: 48.4 us -> 1.67 us
  loops' own time: 14.8 us -> 0 us
  between operations: 13.1 us -> 0.01 us
  matrix products: 12.4 us -> 0 us
  other arithmetic: 12.1 us -> 0 us
    all_gather x2 -> x0, waiting for transfers between devices: 287 us -> none  [the longest x1 144 us: local(): lax.all_gather(values, 'ctx', axis=0, tiled=True)]
    reduce_scatter x1 -> x0, waiting for transfers between devices: 136 us -> none  [local(): lax.psum_scatter(partial_value.astype(jnp.bfloat16), 'head', scatter_dime...]
    pallas_call x0 -> x1, Pallas kernels: none -> 82.9 us  [local(): pl.pallas_call(functools.partial(layer_kernel, nz, ny), out_shape=jax.Sha...]
    gather x18 -> x0, local copies, waits for them, and re-layouts: 41.2 us -> none  [the longest x6 16.7 us: one_turn(): jnp.take(key_blocks, source, axis=0)]
    another operation x3 -> x0, loops' own time: 14.8 us -> none  [the longest x1 10.4 us: local(): attended = lax.map(one_block, jnp.arange(local_blocks, dtype=jnp.int32))]
    dot_general x13 -> x0, matrix products: 12.4 us -> none  [the longest x6 4.92 us: absorb(): jnp.einsum('kgts,skd->kgtd', weights, value_piece, preferred_element_type...]
    dynamic_slice x10 -> x0, local copies, waits for them, and re-layouts: 5.32 us -> none  [the longest x2 2.51 us: one_block(): seq_block = swap_pairs[storage]]
  transfers between devices with their start and end apart: 3 -> 0, of which waited for: 3 -> 0; matrix products, arithmetic and copies ran while one was open for 1% -> 0% of each run, Pallas kernels for 0% -> 0%
where the time goes in v2:
time: 84.7 us; the launch traced here: 84.6 us
  Pallas kernels  82.9 us (98%)
  local copies, waits for them, and re-layouts  1.67 us (2%)
    pallas_call x1, Pallas kernels, local(): pl.pallas_call(functools.partial(layer_kernel, nz, ny), out_shape=jax.Sha...  82.9 us

profile of v2, /device:TPU:1, one launch (start us, length us, event | category | flops | bytes accessed | tf_op | source)
XLA Modules:
  0.0 84.6 jit_solution(1817248930103731713)
XLA Ops:
  0.0 82.9 %layer.1 = bf16[256,512]{1,0:T(8,128)(2,1)} custom-call(s32[128]{0:T(128)} %swap.1, s32[4]{0:T(128)} %docs.1, bf16[256,512]{1,0:T(8,128)(2,1)} %q_ref.1, bf16[256,128]{1,0:T(8,128)(2,1)} %k_ref.1, bf16[256,128]{1,0:T(8,128)(2,1)} %v_ref.1, bf16[512,4096]{1,0:T(8,128)(2,1)} %w_ref.1), custom_call_target="tpu_custom_call" | custom-call | tf_op jit(solution)/shard_map/layer/pallas_call | solution.py:290
  82.9 1.7 %copy.8 = bf16[256,512]{1,0:T(8,128)(2,1)} copy(bf16[256,512]{1,0:T(8,128)(2,1)} %layer.1) | data formatting | bytes 524288

commit v3 on v2

v3 whole, which is shorter than its diff:
```python
import functools

import jax
import jax.numpy as jnp
from jax import lax
from jax.experimental import pallas as pl
from jax.experimental.pallas import tpu as pltpu
from jax.sharding import PartitionSpec as P

HD = 128
BLOCK = 128
NX = 4
NC = 2
PER = 2
ONES = 16
MIRROR = (0, 2, 1, 3)
SCALE2 = 1.4426950408889634 * HD ** (-0.5)
MASKED = -1e30
MESH = pl.DeviceIdType.MESH
ANY = pl.BlockSpec(memory_space=pl.ANY)
VMEM = pl.BlockSpec(memory_space=pltpu.VMEM)
SMEM = pl.BlockSpec(memory_space=pltpu.SMEM)


def layer_kernel(
    nz, ny,
    swap, docs, q_ref, k_ref, v_ref, w_ref, out_ref,
    q_in, v_in, w_all, k_all, v_all, qt, acc, tops,
    o_give, o_take, s_give, s_take, att, given, taken, sums, finals,
    lsem, zsend, zrecv, qsend, qrecv, osend, orecv, ssend, srecv, csend, crecv, ysend, yrecv,
):
    ctx = lax.axis_index("ctx")
    head = lax.axis_index("head")
    z, x = ctx // NX, lax.rem(ctx, NX)
    y, core = head // NC, lax.rem(head, NC)
    zat = lambda zz: lax.rem(zz + nz, nz)
    yat = lambda yy: lax.rem(yy + ny, ny)
    zdev = lambda d: (zat(z + d) * NX + x, head)
    columns = [x, lax.rem(x + 1, NX), lax.rem(x + NX - 1, NX), lax.rem(x + 2, NX)]
    peers = [(z * NX + c, head) for c in columns]
    twin = (ctx, y * NC + 1 - core)
    ydev = lambda yy: (ctx, yat(yy) * NC + core)
    hops = (2, 1, 3)
    stages = nz // 4
    group = qt.shape[2] // BLOCK
    cols = out_ref.shape[1]

    def remote(src, dst, send_sem, recv_sem, device):
        return pltpu.make_async_remote_copy(
            src_ref=src, dst_ref=dst, send_sem=send_sem, recv_sem=recv_sem, device_id=device, device_id_type=MESH
        )

    barrier = pltpu.get_barrier_semaphore()
    friends = [zdev(d) for d in (1, -1, 2, -2)] + peers[1:] + [twin] + [ydev(y + d) for d in hops]
    for device in friends:
        pl.semaphore_signal(barrier, inc=1, device_id=device, device_id_type=MESH)

    loads = [
        pltpu.make_async_copy(q_ref, q_in, lsem.at[0]),
        pltpu.make_async_copy(v_ref, v_in, lsem.at[1]),
        pltpu.make_async_copy(k_ref, k_all.at[z], lsem.at[2]),
        pltpu.make_async_copy(w_ref, w_all, lsem.at[3]),
    ]
    for c in loads:
        c.start()
    loads[1].wait()
    v_all[z] = v_in[...].T
    loads[0].wait()
    for t in range(PER):
        for h in range(group):
            qt[t, :, h * BLOCK:(h + 1) * BLOCK] = q_in[t * BLOCK:(t + 1) * BLOCK, h * HD:(h + 1) * HD].T
    loads[2].wait()
    pl.semaphore_wait(barrier, len(friends))

    def zcopy(stream, way, stage, leap):
        origin = zat(z - 2 * stage) if way == 0 else zat(z + 2 * stage)
        ref = (k_all if stream == 0 else v_all).at[origin]
        sems = (stream, way, stage, leap)
        return remote(ref, ref, zsend.at[sems], zrecv.at[sems], zdev((1 + leap) * (1 if way == 0 else -1)))

    def used(stream, way, stage, leap):
        return stage < stages - 1 or leap == 0 or stream == way

    zall = [
        (stream, way, stage, leap)
        for stage in range(stages) for leap in (1, 0) for stream in (0, 1) for way in (0, 1)
        if used(stream, way, stage, leap)
    ]
    zc = {key: zcopy(*key) for key in zall}
    pick = lambda stage, leap: [key for key in zall if key[2] == stage and key[3] == leap]
    qcopy = [
        [
            remote(qt.at[t], qt.at[PER * MIRROR[p] + t], qsend.at[p - 1, t], qrecv.at[MIRROR[p] - 1, t], peers[p])
            for t in range(PER)
        ]
        for p in range(1, NX)
    ]
    for key in pick(0, 1):
        zc[key].start()
    for p in range(1, NX):
        qcopy[p - 1][0].start()
    for key in pick(0, 0):
        zc[key].start()
    for p in range(1, NX):
        qcopy[p - 1][1].start()

    def arrive(stage):
        for key in pick(stage, 1):
            zc[key].wait_recv()
            onward = key[:2] + (stage + 1, 1)
            if onward in zc:
                zc[onward].start()
        if stage + 1 < stages:
            for key in pick(stage + 1, 0):
                zc[key].start()
        for key in pick(stage, 0):
            zc[key].wait_recv()

    def queries(p, t):
        qcopy[MIRROR[p] - 1][t].wait_recv()

    seqs, starts = [], []
    for j in range(NX * PER):
        seq = swap[(z * NX + columns[j // PER]) * PER + j % PER]
        start = jnp.int32(0)
        end = jnp.int32(0)
        for d in range(docs.shape[0]):
            end = end + docs[d]
            start = jnp.where(end <= seq, end, start)
        seqs.append(seq)
        starts.append(start)

    acc[...] = jnp.zeros_like(acc)
    tops[...] = jnp.full_like(tops, MASKED)
    wide = group * BLOCK
    causal = lax.broadcasted_iota(jnp.int32, (BLOCK, wide), 0) <= lax.rem(
        lax.broadcasted_iota(jnp.int32, (BLOCK, wide), 1), BLOCK
    )

    def absorb(j, chunks, diagonal=False):
        rows, offsets = [], []
        old = tops[j]
        new = old
        for origin in chunks:
            s = jnp.dot(k_all[origin], qt[j], preferred_element_type=jnp.float32)
            for b in range(PER):
                ks = swap[(origin * NX + x) * PER + b]
                seen = (ks >= starts[j]) & (ks <= seqs[j])
                offset = jnp.where(seen, 0.0, MASKED).astype(jnp.float32)
                part = s[b * BLOCK:(b + 1) * BLOCK]
                if diagonal and b == j:
                    part = jnp.where(causal, part, MASKED)
                new = jnp.maximum(new, jnp.max(part, axis=0, keepdims=True) + offset)
                rows.append(part)
                offsets.append(offset)
        level = new * SCALE2
        weights = [
            jnp.exp2(part * SCALE2 - (level - offset)).astype(jnp.bfloat16) for part, offset in zip(rows, offsets)
        ]
        vals = jnp.concatenate([v_all[origin] for origin in chunks], axis=1)
        vals = jnp.concatenate([vals, jnp.ones((ONES, vals.shape[1]), jnp.bfloat16)], axis=0)
        product = jnp.dot(vals, jnp.concatenate(weights, axis=0), preferred_element_type=jnp.float32)
        acc[j] = acc[j] * jnp.exp2((old - new) * SCALE2) + product
        tops[j] = new

    def batch(stage):
        near = [zat(z - 2 * stage - 1), zat(z + 2 * stage + 1), zat(z + 2 * stage + 2)]
        return near + ([zat(z - 2 * stage - 2)] if stage < stages - 1 else [])

    ocopy = [
        [
            remote(
                o_give.at[p - 1, t], o_take.at[MIRROR[p] - 1, t],
                osend.at[p - 1, t], orecv.at[MIRROR[p] - 1, t], peers[p],
            )
            for t in range(PER)
        ]
        for p in range(1, NX)
    ]
    scopy = [
        [
            remote(
                s_give.at[p - 1, t], s_take.at[MIRROR[p] - 1, t],
                ssend.at[p - 1, t], srecv.at[MIRROR[p] - 1, t], peers[p],
            )
            for t in range(PER)
        ]
        for p in range(1, NX)
    ]

    def give(p, t):
        j = PER * p + t
        total = acc[j, HD:HD + 1, :]
        some = total > 0.0
        total = jnp.where(some, total, 1.0)
        s_give[p - 1, t] = jnp.where(some, tops[j] * SCALE2 + jnp.log2(total), MASKED)
        o_give[p - 1, t] = (acc[j, :HD, :] / total).astype(jnp.bfloat16)
        scopy[p - 1][t].start()
        ocopy[p - 1][t].start()

    def product(t, yy, cc):
        at = pl.multiple_of((yat(yy) * NC + cc) * cols, cols)
        return jnp.dot(
            att[t * BLOCK:(t + 1) * BLOCK, :], w_all[:, pl.ds(at, cols)], preferred_element_type=jnp.float32
        )

    order = hops + (0,)
    ccopy = [
        [remote(given.at[t, i], taken.at[t, i], csend.at[t, i], crecv.at[t, i], twin) for i in range(ny)]
        for t in range(PER)
    ]
    ycopy = [
        [
            remote(sums.at[t, i], finals.at[t, i], ysend.at[t, i], yrecv.at[t, i], ydev(y + d))
            for i, d in enumerate(hops)
        ]
        for t in range(PER)
    ]

    def merge(t):
        for p in range(NX - 1):
            scopy[p][t].wait_recv()
            ocopy[p][t].wait_recv()
        levels = [tops[t] * SCALE2 + jnp.log2(acc[t, HD:HD + 1, :])] + [s_take[p, t] for p in range(NX - 1)]
        top = functools.reduce(jnp.maximum, levels)
        shares = [jnp.exp2(v - top) for v in levels]
        whole = functools.reduce(jnp.add, shares)
        mixed = acc[t, :HD, :] * (jnp.exp2(tops[t] * SCALE2 - top) / whole)
        for p in range(NX - 1):
            mixed = mixed + o_take[p, t].astype(jnp.float32) * (shares[p + 1] / whole)
        for h in range(group):
            att[t * BLOCK:(t + 1) * BLOCK, h * HD:(h + 1) * HD] = (
                mixed[:, h * BLOCK:(h + 1) * BLOCK].T.astype(jnp.bfloat16)
            )
        for i, d in enumerate(order):
            given[t, i] = product(t, y + d, 1 - core).astype(jnp.bfloat16)
            ccopy[t][i].start()

    def scatter(t):
        for i, d in enumerate(order):
            total = product(t, y + d, core)
            ccopy[t][i].wait_recv()
            total = total + taken[t, i].astype(jnp.float32)
            if d:
                sums[t, i] = total.astype(jnp.bfloat16)
                ycopy[t][i].start()
            else:
                return total

    def finish(t, total):
        for i in range(len(hops)):
            ycopy[t][i].wait_recv()
            total = total + finals[t, i].astype(jnp.float32)
        out_ref[t * BLOCK:(t + 1) * BLOCK, :] = total.astype(out_ref.dtype)

    own = (0, 1)
    for j in own:
        absorb(j, [z], diagonal=True)
    arrive(0)
    for j in own:
        absorb(j, batch(0))
    for p in (1, 2):
        queries(p, 0)
        absorb(PER * p, [z] + batch(0))
    arrive(1)
    queries(3, 0)
    absorb(PER * 3, [z] + batch(0))
    for p in range(NX):
        absorb(PER * p, batch(1))
    arrive(2)
    for p in range(NX):
        absorb(PER * p, batch(2))
    arrive(3)
    for p in (3, 1, 2):
        absorb(PER * p, batch(3))
        give(p, 0)
    absorb(0, batch(3))
    loads[3].wait()
    for p in (3, 1, 2):
        queries(p, 1)
        absorb(PER * p + 1, [z] + batch(0) + batch(3))
        absorb(PER * p + 1, batch(1) + batch(2))
        give(p, 1)
        if p == 1:
            merge(0)
    first = scatter(0)
    absorb(1, batch(1) + batch(2) + batch(3))
    merge(1)
    second = scatter(1)
    finish(0, first)
    finish(1, second)

    for copies in qcopy + ocopy + scopy + ccopy + ycopy:
        for c in copies:
            c.wait_send()
    for key in zall:
        zc[key].wait_send()


def local(queries, keys, values, out_weight, doc_blocks, swap_pairs, nz, ny):
    toks, feats = queries.shape
    dma = pltpu.SemaphoreType.DMA
    bf = jnp.bfloat16
    f32 = jnp.float32
    cols = out_weight.shape[1] // (ny * NC)
    return pl.pallas_call(
        functools.partial(layer_kernel, nz, ny),
        out_shape=jax.ShapeDtypeStruct((toks, cols), bf),
        in_specs=[SMEM, SMEM, ANY, ANY, ANY, ANY],
        out_specs=VMEM,
        scratch_shapes=[
            pltpu.VMEM((toks, feats), bf),
            pltpu.VMEM((toks, HD), bf),
            pltpu.VMEM(out_weight.shape, bf),
            pltpu.VMEM((nz, toks, HD), bf),
            pltpu.VMEM((nz, HD, toks), bf),
            pltpu.VMEM((NX * PER, HD, feats), bf),
            pltpu.VMEM((NX * PER, HD + ONES, feats), f32),
            pltpu.VMEM((NX * PER, 1, feats), f32),
            pltpu.VMEM((NX - 1, PER, HD, feats), bf),
            pltpu.VMEM((NX - 1, PER, HD, feats), bf),
            pltpu.VMEM((NX - 1, PER, 1, feats), f32),
            pltpu.VMEM((NX - 1, PER, 1, feats), f32),
            pltpu.VMEM((toks, feats), bf),
            pltpu.VMEM((PER, ny, BLOCK, cols), bf),
            pltpu.VMEM((PER, ny, BLOCK, cols), bf),
            pltpu.VMEM((PER, ny - 1, BLOCK, cols), bf),
            pltpu.VMEM((PER, ny - 1, BLOCK, cols), bf),
            dma((4,)), dma((2, 2, nz // 4, 2)), dma((2, 2, nz // 4, 2)),
            dma((NX - 1, PER)), dma((NX - 1, PER)), dma((NX - 1, PER)), dma((NX - 1, PER)),
            dma((NX - 1, PER)), dma((NX - 1, PER)),
            dma((PER, ny)), dma((PER, ny)), dma((PER, ny - 1)), dma((PER, ny - 1)),
        ],
        compiler_params=pltpu.CompilerParams(
            collective_id=0, has_side_effects=True, vmem_limit_bytes=56 << 20
        ),
        name="layer",
    )(swap_pairs, doc_blocks, queries, keys, values, out_weight)


def solution(mesh):
    nz = mesh.shape["ctx"] // NX
    ny = mesh.shape["head"] // NC
    in_specs = (P("ctx", "head"), P("ctx", "head"), P("ctx", "head"), P("head", None), P(), P())
    return jax.shard_map(
        functools.partial(local, nz=nz, ny=ny),
        mesh=mesh, in_specs=in_specs, out_specs=P("ctx", "head"), check_vma=False,
    )
```

time: 84.7 us -> 79.6 us (0.940)
  Pallas kernels: 82.9 us -> 77.3 us
    pallas_call x1, Pallas kernels: 82.9 us -> 77.3 us  [local(): pl.pallas_call(functools.partial(layer_kernel, nz, ny), out_shape=jax.Sha...]
where the time goes in v3:
time: 79.6 us; the launch traced here: 79 us
  Pallas kernels  77.3 us (97%)
  local copies, waits for them, and re-layouts  1.67 us (2%)
    pallas_call x1, Pallas kernels, local(): pl.pallas_call(functools.partial(layer_kernel, nz, ny), out_shape=jax.Sha...  77.3 us
    unnamed x1, local copies, waits for them, and re-layouts  1.67 us

profile of v3, /device:TPU:1, one launch (start us, length us, event | category | flops | bytes accessed | tf_op | source)
XLA Modules:
  0.0 79.0 jit_solution(15412424244883333785)
XLA Ops:
  0.0 77.3 %layer.1 = bf16[256,512]{1,0:T(8,128)(2,1)} custom-call(s32[128]{0:T(128)} %swap.1, s32[4]{0:T(128)} %docs.1, bf16[256,512]{1,0:T(8,128)(2,1)} %q_ref.1, bf16[256,128]{1,0:T(8,128)(2,1)} %k_ref.1, bf16[256,128]{1,0:T(8,128)(2,1)} %v_ref.1, bf16[512,4096]{1,0:T(8,128)(2,1)} %w_ref.1), custom_call_target="tpu_custom_call" | custom-call | tf_op jit(solution)/shard_map/layer/pallas_call | solution.py:306
  77.3 1.7 %copy.8 = bf16[256,512]{1,0:T(8,128)(2,1)} copy(bf16[256,512]{1,0:T(8,128)(2,1)} %layer.1) | data formatting | bytes 524288

commit v4 on v3

v4 whole, which is shorter than its diff:
```python
import functools

import jax
import jax.numpy as jnp
from jax import lax
from jax.experimental import pallas as pl
from jax.experimental.pallas import tpu as pltpu
from jax.sharding import PartitionSpec as P

HD = 128
BLOCK = 128
NX = 4
NC = 2
PER = 2
ONES = 16
SPLIT = 2
PARTS = 2
SUB = BLOCK // PARTS
MIRROR = (0, 2, 1, 3)
SCALE2 = 1.4426950408889634 * HD ** (-0.5)
MASKED = -1e30
MESH = pl.DeviceIdType.MESH
ANY = pl.BlockSpec(memory_space=pl.ANY)
VMEM = pl.BlockSpec(memory_space=pltpu.VMEM)
SMEM = pl.BlockSpec(memory_space=pltpu.SMEM)


def layer_kernel(
    nz, ny,
    swap, docs, q_ref, k_ref, v_ref, w_ref, out_ref,
    q_in, v_in, w_all, k_all, v_all, qt, acc, tops,
    o_give, o_take, s_give, s_take, att, given, taken, sums, finals, kept,
    lsem, zsend, zrecv, qsend, qrecv, osend, orecv, ssend, srecv, csend, crecv, ysend, yrecv,
):
    ctx = lax.axis_index("ctx")
    head = lax.axis_index("head")
    z, x = ctx // NX, lax.rem(ctx, NX)
    y, core = head // NC, lax.rem(head, NC)
    zat = lambda zz: lax.rem(zz + nz, nz)
    yat = lambda yy: lax.rem(yy + ny, ny)
    zdev = lambda d: (zat(z + d) * NX + x, head)
    columns = [x, lax.rem(x + 1, NX), lax.rem(x + NX - 1, NX), lax.rem(x + 2, NX)]
    peers = [(z * NX + c, head) for c in columns]
    twin = (ctx, y * NC + 1 - core)
    ydev = lambda yy: (ctx, yat(yy) * NC + core)
    hops = (2, 1, 3)
    far = nz // 2
    group = qt.shape[2] // BLOCK
    cols = out_ref.shape[1]

    def remote(src, dst, send_sem, recv_sem, device):
        return pltpu.make_async_remote_copy(
            src_ref=src, dst_ref=dst, send_sem=send_sem, recv_sem=recv_sem, device_id=device, device_id_type=MESH
        )

    barrier = pltpu.get_barrier_semaphore()
    friends = [zdev(d) for d in (1, -1)] + peers[1:] + [twin] + [ydev(y + d) for d in hops]
    for device in friends:
        pl.semaphore_signal(barrier, inc=1, device_id=device, device_id_type=MESH)

    loads = [
        pltpu.make_async_copy(q_ref, q_in, lsem.at[0]),
        pltpu.make_async_copy(v_ref, v_in, lsem.at[1]),
        pltpu.make_async_copy(k_ref, k_all.at[z], lsem.at[2]),
        pltpu.make_async_copy(w_ref, w_all, lsem.at[3]),
    ]
    for c in loads:
        c.start()
    loads[1].wait()
    v_all[z] = v_in[...].T
    loads[0].wait()
    for t in range(PER):
        for h in range(group):
            turned = q_in[t * BLOCK:(t + 1) * BLOCK, h * HD:(h + 1) * HD].T
            for u in range(PARTS):
                qt[t, :, (u * group + h) * SUB:(u * group + h + 1) * SUB] = turned[:, u * SUB:(u + 1) * SUB]
    loads[2].wait()
    pl.semaphore_wait(barrier, len(friends))

    def zcopy(stream, way, step):
        origin = zat(z - step) if way == 0 else zat(z + step)
        ref = k_all if stream < SPLIT else v_all
        size = ref.shape[1] // SPLIT
        ref = ref.at[origin, pl.ds(stream % SPLIT * size, size)]
        sems = (stream, way, step)
        return remote(ref, ref, zsend.at[sems], zrecv.at[sems], zdev(1 if way == 0 else -1))

    zall = [
        (stream, way, step)
        for step in range(far) for stream in range(2 * SPLIT) for way in (0, 1)
        if step < far - 1 or (stream < SPLIT) == (way == 0)
    ]
    zc = {key: zcopy(*key) for key in zall}
    pick = lambda step: [key for key in zall if key[2] == step]
    qcopy = [
        [
            remote(qt.at[t], qt.at[PER * MIRROR[p] + t], qsend.at[p - 1, t], qrecv.at[MIRROR[p] - 1, t], peers[p])
            for t in range(PER)
        ]
        for p in range(1, NX)
    ]
    for key in pick(0):
        zc[key].start()
    for p in (1, 2, 3):
        qcopy[p - 1][0].start()

    def arrive(step, streams=range(2 * SPLIT)):
        for key in pick(step):
            if key[0] not in streams:
                continue
            zc[key].wait_recv()
            onward = key[:2] + (step + 1,)
            if onward in zc:
                zc[onward].start()

    def queries(p, t):
        qcopy[MIRROR[p] - 1][t].wait_recv()

    seqs, starts = [], []
    for j in range(NX * PER):
        seq = swap[(z * NX + columns[j // PER]) * PER + j % PER]
        start = jnp.int32(0)
        end = jnp.int32(0)
        for d in range(docs.shape[0]):
            end = end + docs[d]
            start = jnp.where(end <= seq, end, start)
        seqs.append(seq)
        starts.append(start)

    acc[...] = jnp.zeros_like(acc)
    tops[...] = jnp.full_like(tops, MASKED)
    wide = group * SUB
    lane = lax.broadcasted_iota(jnp.int32, (BLOCK, PARTS * wide), 1)
    causal = lax.broadcasted_iota(jnp.int32, (BLOCK, PARTS * wide), 0) <= lane // wide * SUB + lax.rem(lane, SUB)

    def score(j, chunks, diagonal=False):
        rows, offsets = [], []
        new = tops[j]
        for origin in chunks:
            s = jnp.dot(k_all[origin], qt[j], preferred_element_type=jnp.float32)
            for b in range(PER):
                ks = swap[(origin * NX + x) * PER + b]
                seen = (ks >= starts[j]) & (ks <= seqs[j])
                offset = jnp.where(seen, 0.0, MASKED).astype(jnp.float32)
                part = s[b * BLOCK:(b + 1) * BLOCK]
                if diagonal and b == j:
                    part = jnp.where(causal, part, MASKED)
                new = jnp.maximum(new, jnp.max(part, axis=0, keepdims=True) + offset)
                rows.append(part)
                offsets.append(offset)
        return j, chunks, rows, offsets, new

    def absorb(j, chunks, rows, offsets, new):
        level = new * SCALE2
        weights = [
            jnp.exp2(part * SCALE2 - (level - offset)).astype(jnp.bfloat16) for part, offset in zip(rows, offsets)
        ]
        vals = jnp.concatenate([v_all[origin] for origin in chunks], axis=1)
        vals = jnp.concatenate([vals, jnp.ones((ONES, vals.shape[1]), jnp.bfloat16)], axis=0)
        product = jnp.dot(vals, jnp.concatenate(weights, axis=0), preferred_element_type=jnp.float32)
        acc[j] = acc[j] * jnp.exp2((tops[j] - new) * SCALE2) + product
        tops[j] = new

    def attend(units, done=lambda p, t: None):
        ask = lambda p, t, rows: score(PER * p + t, [c for r in rows for c in row(r)])
        asked = ask(*units[0])
        for n, (p, t, _) in enumerate(units):
            ahead = ask(*units[n + 1]) if n + 1 < len(units) else None
            absorb(*asked)
            done(p, t)
            asked = ahead

    def row(step):
        if step < 0:
            return [z]
        return [zat(z - 1 - step), zat(z + 1 + step)] if step < far - 1 else [zat(z + far)]

    pieces = [(t, u) for t in range(PER) for u in range(PARTS)]

    def back(give_ref, take_ref, sends, recvs, p, i):
        m = MIRROR[p] - 1
        return remote(
            give_ref.at[p - 1, i], take_ref.at[m, i], sends.at[p - 1, i], recvs.at[m, i], peers[p]
        )

    ocopy = [[back(o_give, o_take, osend, orecv, p, i) for i in range(len(pieces))] for p in range(1, NX)]
    scopy = [[back(s_give, s_take, ssend, srecv, p, i) for i in range(len(pieces))] for p in range(1, NX)]

    def give(p, i):
        t, u = pieces[i]
        j = PER * p + t
        lanes = slice(u * wide, (u + 1) * wide)
        total = acc[j, HD:HD + 1, lanes]
        some = total > 0.0
        total = jnp.where(some, total, 1.0)
        s_give[p - 1, i] = jnp.where(some, tops[j, :, lanes] * SCALE2 + jnp.log2(total), MASKED)
        o_give[p - 1, i] = (acc[j, :HD, lanes] / total).astype(jnp.bfloat16)
        scopy[p - 1][i].start()
        ocopy[p - 1][i].start()

    def product(i, yy, cc):
        at = pl.multiple_of((yat(yy) * NC + cc) * cols, cols)
        return jnp.dot(att[i * SUB:(i + 1) * SUB, :], w_all[:, pl.ds(at, cols)], preferred_element_type=jnp.float32)

    order = hops + (0,)
    ccopy = [
        [remote(given.at[i, n], taken.at[i, n], csend.at[i, n], crecv.at[i, n], twin) for n in range(ny)]
        for i in range(len(pieces))
    ]
    ycopy = [
        [
            remote(sums.at[i, n], finals.at[i, n], ysend.at[i, n], yrecv.at[i, n], ydev(y + d))
            for n, d in enumerate(hops)
        ]
        for i in range(len(pieces))
    ]

    def merge(i):
        t, u = pieces[i]
        lanes = slice(u * wide, (u + 1) * wide)
        for p in range(NX - 1):
            scopy[p][i].wait_recv()
            ocopy[p][i].wait_recv()
        own_level = tops[t, :, lanes] * SCALE2
        levels = [own_level + jnp.log2(acc[t, HD:HD + 1, lanes])] + [s_take[p, i] for p in range(NX - 1)]
        top = functools.reduce(jnp.maximum, levels)
        shares = [jnp.exp2(v - top) for v in levels]
        whole = functools.reduce(jnp.add, shares)
        mixed = acc[t, :HD, lanes] * (jnp.exp2(own_level - top) / whole)
        for p in range(NX - 1):
            mixed = mixed + o_take[p, i].astype(jnp.float32) * (shares[p + 1] / whole)
        for h in range(group):
            att[i * SUB:(i + 1) * SUB, h * HD:(h + 1) * HD] = (
                mixed[:, h * SUB:(h + 1) * SUB].T.astype(jnp.bfloat16)
            )
        for n, d in enumerate(order):
            given[i, n] = product(i, y + d, 1 - core).astype(jnp.bfloat16)
            ccopy[i][n].start()

    def scatter(i):
        for n, d in enumerate(order):
            total = product(i, y + d, core)
            ccopy[i][n].wait_recv()
            total = total + taken[i, n].astype(jnp.float32)
            if d:
                sums[i, n] = total.astype(jnp.bfloat16)
                ycopy[i][n].start()
            else:
                kept[i] = total

    def finish(i):
        total = kept[i]
        for n in range(len(hops)):
            ycopy[i][n].wait_recv()
            total = total + finals[i, n].astype(jnp.float32)
        out_ref[i * SUB:(i + 1) * SUB, :] = total.astype(out_ref.dtype)

    last = far - 1
    table = [
        [(0, 0, [0]), (0, 1, [0])],
        [(1, 0, [-1, 0, 1]), (2, 0, [-1, 0, 1]), (0, 0, [1])],
        [(3, 0, [-1, 0, 1, 2]), (1, 1, [-1, 0, 1, 2]), (2, 1, [-1, 0, 1, 2])],
        [(3, 1, [-1, 0, 1, 2, 3]), (0, 0, [2, 3]), (0, 1, [1, 2, 3])],
        [(1, 0, [2, 3, 4]), (2, 0, [2, 3, 4]), (3, 0, [3, 4])],
        [(1, 1, [3, 4, 5]), (2, 1, [3, 4, 5]), (3, 1, [4, 5])],
        [(3, 0, [5, 6]), (1, 0, [5, 6]), (2, 0, [5, 6]), (0, 0, [4, 5, 6])],
    ]
    for t in range(PER):
        absorb(*score(t, [z], diagonal=True))

    def second_half(p):
        qcopy[p - 1][0].wait_send()
        qcopy[p - 1][1].start()

    second_half(1)
    second_half(2)
    asked = set()
    for step, units in enumerate(table):
        arrive(step)
        if step == 0:
            second_half(3)
        for p, t, _ in units:
            if p and (p, t) not in asked:
                queries(p, t)
                asked.add((p, t))
        attend(units)
    arrive(last)

    def done(p, t):
        for u in range(PARTS if t == 0 else 1):
            if p:
                give(p, PARTS * t + u)

    ends = [(p, 0, [last]) for p in (3, 1, 2, 0)] + [(p, 1, [last - 1, last]) for p in (3, 1, 2)]
    attend(ends + [(0, 1, [last - 3, last - 2, last - 1, last])], done)
    for p in (3, 1, 2):
        for u in range(1, PARTS):
            give(p, PARTS + u)
    loads[3].wait()
    for i in range(len(pieces)):
        merge(i)
        if i:
            scatter(i - 1)
    scatter(len(pieces) - 1)
    for i in range(len(pieces)):
        finish(i)

    for c in [copies[1] for copies in qcopy]:
        c.wait_send()
    for copies in ocopy + scopy + ccopy + ycopy:
        for c in copies:
            c.wait_send()
    for key in zall:
        zc[key].wait_send()


def local(queries, keys, values, out_weight, doc_blocks, swap_pairs, nz, ny):
    toks, feats = queries.shape
    dma = pltpu.SemaphoreType.DMA
    bf = jnp.bfloat16
    f32 = jnp.float32
    cols = out_weight.shape[1] // (ny * NC)
    parts = PER * PARTS
    return pl.pallas_call(
        functools.partial(layer_kernel, nz, ny),
        out_shape=jax.ShapeDtypeStruct((toks, cols), bf),
        in_specs=[SMEM, SMEM, ANY, ANY, ANY, ANY],
        out_specs=VMEM,
        scratch_shapes=[
            pltpu.VMEM((toks, feats), bf),
            pltpu.VMEM((toks, HD), bf),
            pltpu.VMEM(out_weight.shape, bf),
            pltpu.VMEM((nz, toks, HD), bf),
            pltpu.VMEM((nz, HD, toks), bf),
            pltpu.VMEM((NX * PER, HD, feats), bf),
            pltpu.VMEM((NX * PER, HD + ONES, feats), f32),
            pltpu.VMEM((NX * PER, 1, feats), f32),
            pltpu.VMEM((NX - 1, parts, HD, feats // PARTS), bf),
            pltpu.VMEM((NX - 1, parts, HD, feats // PARTS), bf),
            pltpu.VMEM((NX - 1, parts, 1, feats // PARTS), f32),
            pltpu.VMEM((NX - 1, parts, 1, feats // PARTS), f32),
            pltpu.VMEM((toks, feats), bf),
            pltpu.VMEM((parts, ny, SUB, cols), bf),
            pltpu.VMEM((parts, ny, SUB, cols), bf),
            pltpu.VMEM((parts, ny - 1, SUB, cols), bf),
            pltpu.VMEM((parts, ny - 1, SUB, cols), bf),
            pltpu.VMEM((parts, SUB, cols), f32),
            dma((4,)), dma((2 * SPLIT, 2, nz // 2)), dma((2 * SPLIT, 2, nz // 2)),
            dma((NX - 1, PER)), dma((NX - 1, PER)),
            dma((NX - 1, parts)), dma((NX - 1, parts)), dma((NX - 1, parts)), dma((NX - 1, parts)),
            dma((parts, ny)), dma((parts, ny)), dma((parts, ny - 1)), dma((parts, ny - 1)),
        ],
        compiler_params=pltpu.CompilerParams(
            collective_id=0, has_side_effects=True, vmem_limit_bytes=56 << 20
        ),
        name="layer",
    )(swap_pairs, doc_blocks, queries, keys, values, out_weight)


def solution(mesh):
    nz = mesh.shape["ctx"] // NX
    ny = mesh.shape["head"] // NC
    in_specs = (P("ctx", "head"), P("ctx", "head"), P("ctx", "head"), P("head", None), P(), P())
    return jax.shard_map(
        functools.partial(local, nz=nz, ny=ny),
        mesh=mesh, in_specs=in_specs, out_specs=P("ctx", "head"), check_vma=False,
    )
```

time: 79.6 us -> 73.5 us (0.923)
  Pallas kernels: 77.3 us -> 71.6 us
    pallas_call x1, Pallas kernels: 77.3 us -> 71.6 us  [local(): pl.pallas_call(functools.partial(layer_kernel, nz, ny), out_shape=jax.Sha...]
where the time goes in v4:
time: 73.5 us; the launch traced here: 73.3 us
  Pallas kernels  71.6 us (97%)
  local copies, waits for them, and re-layouts  1.67 us (2%)
    pallas_call x1, Pallas kernels, local(): pl.pallas_call(functools.partial(layer_kernel, nz, ny), out_shape=jax.Sha...  71.6 us
    unnamed x1, local copies, waits for them, and re-layouts  1.67 us

profile of v4, /device:TPU:1, one launch (start us, length us, event | category | flops | bytes accessed | tf_op | source)
XLA Modules:
  0.0 73.3 jit_solution(6185886315366027123)
XLA Ops:
  0.0 71.6 %layer.1 = bf16[256,512]{1,0:T(8,128)(2,1)} custom-call(s32[128]{0:T(128)} %swap.1, s32[4]{0:T(128)} %docs.1, bf16[256,512]{1,0:T(8,128)(2,1)} %q_ref.1, bf16[256,128]{1,0:T(8,128)(2,1)} %k_ref.1, bf16[256,128]{1,0:T(8,128)(2,1)} %v_ref.1, bf16[512,4096]{1,0:T(8,128)(2,1)} %w_ref.1), custom_call_target="tpu_custom_call" | custom-call | tf_op jit(solution)/shard_map/layer/pallas_call | solution.py:324
  71.6 1.7 %copy.8 = bf16[256,512]{1,0:T(8,128)(2,1)} copy(bf16[256,512]{1,0:T(8,128)(2,1)} %layer.1) | data formatting | bytes 524288

commit v5 on v4

--- a/solution.py
+++ b/solution.py
@@ -165,10 +165,12 @@
         ask = lambda p, t, rows: score(PER * p + t, [c for r in rows for c in row(r)])
         asked = ask(*units[0])
         for n, (p, t, _) in enumerate(units):
-            ahead = ask(*units[n + 1]) if n + 1 < len(units) else None
+            more = units[n + 1:n + 2]
+            early = [u for u in more if u[:2] != (p, t)]
+            ahead = ask(*early[0]) if early else None
             absorb(*asked)
             done(p, t)
-            asked = ahead
+            asked = ask(*more[0]) if more and not early else ahead
 
     def row(step):
         if step < 0:
@@ -260,10 +262,10 @@
         [(0, 0, [0]), (0, 1, [0])],
         [(1, 0, [-1, 0, 1]), (2, 0, [-1, 0, 1]), (0, 0, [1])],
         [(3, 0, [-1, 0, 1, 2]), (1, 1, [-1, 0, 1, 2]), (2, 1, [-1, 0, 1, 2])],
-        [(3, 1, [-1, 0, 1, 2, 3]), (0, 0, [2, 3]), (0, 1, [1, 2, 3])],
+        [(3, 1, [-1, 0, 1, 2, 3])],
         [(1, 0, [2, 3, 4]), (2, 0, [2, 3, 4]), (3, 0, [3, 4])],
         [(1, 1, [3, 4, 5]), (2, 1, [3, 4, 5]), (3, 1, [4, 5])],
-        [(3, 0, [5, 6]), (1, 0, [5, 6]), (2, 0, [5, 6]), (0, 0, [4, 5, 6])],
+        [(3, 0, [5, 6]), (1, 0, [5, 6]), (2, 0, [5, 6])],
     ]
     for t in range(PER):
         absorb(*score(t, [z], diagonal=True))
@@ -287,15 +289,19 @@
     arrive(last)
 
     def done(p, t):
-        for u in range(PARTS if t == 0 else 1):
-            if p:
-                give(p, PARTS * t + u)
-
-    ends = [(p, 0, [last]) for p in (3, 1, 2, 0)] + [(p, 1, [last - 1, last]) for p in (3, 1, 2)]
-    attend(ends + [(0, 1, [last - 3, last - 2, last - 1, last])], done)
-    for p in (3, 1, 2):
-        for u in range(1, PARTS):
-            give(p, PARTS + u)
+        if p and t == 0:
+            for u in range(PARTS):
+                give(p, u)
+        elif p:
+            give(p, PARTS)
+        if (p, t) == (2, 1):
+            for u in range(1, PARTS):
+                for peer in (3, 1, 2):
+                    give(peer, PARTS + u)
+
+    ends = [(p, 0, [last]) for p in (3, 1, 2)] + [(p, 1, [last - 1, last]) for p in (3, 1, 2)]
+    ends += [(0, 0, [2, 3, 4]), (0, 1, [1, 2, 3, 4]), (0, 0, [5, 6, last]), (0, 1, [5, 6, last])]
+    attend(ends, done)
     loads[3].wait()
     for i in range(len(pieces)):
         merge(i)

time: 73.5 us -> 75.5 us (1.027)
  Pallas kernels: 71.6 us -> 73.6 us
    pallas_call x1, Pallas kernels: 71.6 us -> 73.6 us  [local(): pl.pallas_call(functools.partial(layer_kernel, nz, ny), out_shape=jax.Sha...]
where the time goes in v5:
time: 75.5 us; the launch traced here: 75.3 us
  Pallas kernels  73.6 us (97%)
  local copies, waits for them, and re-layouts  1.67 us (2%)
    pallas_call x1, Pallas kernels, local(): pl.pallas_call(functools.partial(layer_kernel, nz, ny), out_shape=jax.Sha...  73.6 us
    unnamed x1, local copies, waits for them, and re-layouts  1.67 us

profile of v5, /device:TPU:1, one launch (start us, length us, event | category | flops | bytes accessed | tf_op | source)
XLA Modules:
  0.0 75.3 jit_solution(16128590080994667364)
XLA Ops:
  0.0 73.6 %layer.1 = bf16[256,512]{1,0:T(8,128)(2,1)} custom-call(s32[128]{0:T(128)} %swap.1, s32[4]{0:T(128)} %docs.1, bf16[256,512]{1,0:T(8,128)(2,1)} %q_ref.1, bf16[256,128]{1,0:T(8,128)(2,1)} %k_ref.1, bf16[256,128]{1,0:T(8,128)(2,1)} %v_ref.1, bf16[512,4096]{1,0:T(8,128)(2,1)} %w_ref.1), custom_call_target="tpu_custom_call" | custom-call | tf_op jit(solution)/shard_map/layer/pallas_call | solution.py:330
  73.6 1.7 %copy.8 = bf16[256,512]{1,0:T(8,128)(2,1)} copy(bf16[256,512]{1,0:T(8,128)(2,1)} %layer.1) | data formatting | bytes 524288

commit v6 on v5

--- a/solution.py
+++ b/solution.py
@@ -165,12 +165,10 @@
         ask = lambda p, t, rows: score(PER * p + t, [c for r in rows for c in row(r)])
         asked = ask(*units[0])
         for n, (p, t, _) in enumerate(units):
-            more = units[n + 1:n + 2]
-            early = [u for u in more if u[:2] != (p, t)]
-            ahead = ask(*early[0]) if early else None
+            ahead = ask(*units[n + 1]) if n + 1 < len(units) else None
             absorb(*asked)
             done(p, t)
-            asked = ask(*more[0]) if more and not early else ahead
+            asked = ahead
 
     def row(step):
         if step < 0:
@@ -262,10 +260,10 @@
         [(0, 0, [0]), (0, 1, [0])],
         [(1, 0, [-1, 0, 1]), (2, 0, [-1, 0, 1]), (0, 0, [1])],
         [(3, 0, [-1, 0, 1, 2]), (1, 1, [-1, 0, 1, 2]), (2, 1, [-1, 0, 1, 2])],
-        [(3, 1, [-1, 0, 1, 2, 3])],
+        [(3, 1, [-1, 0, 1, 2, 3]), (0, 0, [2, 3]), (0, 1, [1, 2, 3])],
         [(1, 0, [2, 3, 4]), (2, 0, [2, 3, 4]), (3, 0, [3, 4])],
-        [(1, 1, [3, 4, 5]), (2, 1, [3, 4, 5]), (3, 1, [4, 5])],
-        [(3, 0, [5, 6]), (1, 0, [5, 6]), (2, 0, [5, 6])],
+        [(1, 1, [3, 4, 5]), (2, 1, [3, 4, 5]), (3, 1, [4, 5]), (0, 1, [4, 5])],
+        [(3, 0, [5, 6]), (1, 0, [5, 6]), (2, 0, [5, 6]), (0, 0, [4, 5, 6])],
     ]
     for t in range(PER):
         absorb(*score(t, [z], diagonal=True))
@@ -299,8 +297,7 @@
                 for peer in (3, 1, 2):
                     give(peer, PARTS + u)
 
-    ends = [(p, 0, [last]) for p in (3, 1, 2)] + [(p, 1, [last - 1, last]) for p in (3, 1, 2)]
-    ends += [(0, 0, [2, 3, 4]), (0, 1, [1, 2, 3, 4]), (0, 0, [5, 6, last]), (0, 1, [5, 6, last])]
+    ends = [(p, 0, [last]) for p in (3, 1, 2, 0)] + [(p, 1, [last - 1, last]) for p in (3, 1, 2, 0)]
     attend(ends, done)
     loads[3].wait()
     for i in range(len(pieces)):

time: 75.5 us -> 74.8 us (level)
  no operation moved by 1% of the time
where the time goes in v6:
time: 74.8 us; the launch traced here: 74.6 us
  Pallas kernels  73 us (98%)
  local copies, waits for them, and re-layouts  1.67 us (2%)
    pallas_call x1, Pallas kernels, local(): pl.pallas_call(functools.partial(layer_kernel, nz, ny), out_shape=jax.Sha...  73 us
    unnamed x1, local copies, waits for them, and re-layouts  1.67 us

profile of v6, /device:TPU:1, one launch (start us, length us, event | category | flops | bytes accessed | tf_op | source)
XLA Modules:
  0.0 74.6 jit_solution(9131097296437077299)
XLA Ops:
  0.0 73.0 %layer.1 = bf16[256,512]{1,0:T(8,128)(2,1)} custom-call(s32[128]{0:T(128)} %swap.1, s32[4]{0:T(128)} %docs.1, bf16[256,512]{1,0:T(8,128)(2,1)} %q_ref.1, bf16[256,128]{1,0:T(8,128)(2,1)} %k_ref.1, bf16[256,128]{1,0:T(8,128)(2,1)} %v_ref.1, bf16[512,4096]{1,0:T(8,128)(2,1)} %w_ref.1), custom_call_target="tpu_custom_call" | custom-call | tf_op jit(solution)/shard_map/layer/pallas_call | solution.py:327
  73.0 1.7 %copy.8 = bf16[256,512]{1,0:T(8,128)(2,1)} copy(bf16[256,512]{1,0:T(8,128)(2,1)} %layer.1) | data formatting | bytes 524288
